TPU v7x, 32 devices: a whole 2x2x4 slice. The times are simulated.
32 devices in a mesh: dp: 8 (over z, x), seq: 4 (over y, core).
Axes of the slice: x: 2, y: 2, z: 4, core: 2. Of those that a mesh axis runs over, the one named last changes fastest.
Arguments:
- inputs: bfloat16 [192, 1024, 512], P('dp', 'seq'), may hold values from -6 to 6
- lengths: int32 [192], P('dp'), may hold values from 256 to 1024, as said below
- cotangent: bfloat16 [192, 1024, 512], P('dp', 'seq'), may hold values from -6 to 6
- w_query: bfloat16 [512, 512], P(('dp', 'seq')), may hold values from -0.25 to 0.25
- w_key: bfloat16 [512, 512], P(('dp', 'seq')), may hold values from -0.25 to 0.25
- w_value: bfloat16 [512, 512], P(('dp', 'seq')), may hold values from -0.25 to 0.25
- w_out: bfloat16 [512, 512], P(('dp', 'seq')), may hold values from -0.5 to 0.5
- w_up: bfloat16 [512, 2048], P(('dp', 'seq')), may hold values from -0.25 to 0.25
- w_down: bfloat16 [2048, 512], P(('dp', 'seq')), may hold values from -0.125 to 0.125
- gain_attn: bfloat16 [512], P(('dp', 'seq')), may hold values from 0.25 to 1.75
- gain_mlp: bfloat16 [512], P(('dp', 'seq')), may hold values from 0.25 to 1.75
Outputs:
- output: bfloat16 [192, 1024, 512], P('dp', 'seq')
- grad_input: float32 [192, 1024, 512], P('dp', 'seq')
- grad_query: float32 [512, 512], P(('dp', 'seq'))
- grad_key: float32 [512, 512], P(('dp', 'seq'))
- grad_value: float32 [512, 512], P(('dp', 'seq'))
- grad_out: float32 [512, 512], P(('dp', 'seq'))
- grad_up: float32 [512, 2048], P(('dp', 'seq'))
- grad_down: float32 [2048, 512], P(('dp', 'seq'))
- grad_gain_attn: float32 [512], P(('dp', 'seq'))
- grad_gain_mlp: float32 [512], P(('dp', 'seq'))
Inputs may be any that keep to these rules, and one draw needn't show every extreme that they name: Sequence b's valid slots are its first lengths[b]; some sequence has 1024 of them and some has 256.
All inputs are finite; a program needn't handle non-finite values.
Results may differ from a plain program's by a relative error of at most 0.012.
Values may be sent and summed in bfloat16 or wider, within the bound.
A program may use at most 320 MiB of HBM per device.

v0:
```python
from functools import partial
import math
import jax
import jax.numpy as jnp
from jax import lax
from jax.sharding import PartitionSpec as P

H = 8
HD = 64
SPAN = 128


def normed(values, gain_vec):
    return values * lax.rsqrt(jnp.mean(values * values, axis=-1, keepdims=True) + 1e-06) * gain_vec


def span_scores(query_blk, key_blk, key_sum, first_span):
    seq_group, slots_dev, model_width = query_blk.shape
    spans_dev = slots_dev // SPAN
    span_total = key_sum.shape[1]
    query_h = query_blk.reshape(seq_group, spans_dev, SPAN, H, HD)
    key_h = key_blk.reshape(seq_group, spans_dev, SPAN, H, HD)
    key_sh = key_sum.reshape(seq_group, span_total, H, HD)
    near_score = jnp.einsum(
        "bsihd,bsjhd->bshij", query_h, key_h, preferred_element_type=jnp.float32
    ) * HD ** (-0.5)
    far_score = jnp.einsum(
        "bsihd,bthd->bshit", query_h, key_sh, preferred_element_type=jnp.float32
    ) * HD ** (-0.5)
    row_index = lax.broadcasted_iota(jnp.int32, (SPAN, SPAN), 0)
    col_index = lax.broadcasted_iota(jnp.int32, (SPAN, SPAN), 1)
    causal = row_index >= col_index
    span_here = first_span + jnp.arange(spans_dev, dtype=jnp.int32)
    earlier = (jnp.arange(span_total, dtype=jnp.int32)[None, :] < span_here[:, None])[
        :, None, None, :
    ]
    near_score = jnp.where(causal, near_score, -1e30)
    far_score = jnp.where(earlier, far_score, -1e30)
    return (query_h, key_h, key_sh, near_score, far_score, causal, earlier)


def attend_forward(first_span, entry):
    query_blk, key_blk, value_blk, key_sum, value_sum = entry
    query_h, key_h, key_sh, near_score, far_score, causal, earlier = span_scores(
        query_blk, key_blk, key_sum, first_span
    )
    value_h = value_blk.reshape(key_h.shape)
    value_sh = value_sum.reshape(key_sh.shape)
    highest = jnp.maximum(
        jnp.max(near_score, axis=-1, keepdims=True), jnp.max(far_score, axis=-1, keepdims=True)
    )
    near_exp = jnp.exp(near_score - highest)
    far_exp = jnp.exp(far_score - highest)
    denom_sum = jnp.sum(near_exp, axis=-1, keepdims=True) + jnp.sum(far_exp, axis=-1, keepdims=True)
    near_prob = (near_exp / denom_sum).astype(jnp.bfloat16)
    far_prob = (far_exp / denom_sum).astype(jnp.bfloat16)
    attended = jnp.einsum(
        "bshij,bsjhd->bsihd", near_prob, value_h, preferred_element_type=jnp.float32
    )
    attended = attended + jnp.einsum(
        "bshit,bthd->bsihd", far_prob, value_sh, preferred_element_type=jnp.float32
    )
    return (attended.reshape(query_blk.shape).astype(jnp.bfloat16), highest + jnp.log(denom_sum))


def attend_backward(first_span, entry):
    query_blk, key_blk, value_blk, key_sum, value_sum, log_total, grad_att = entry
    query_h, key_h, key_sh, near_score, far_score, causal, earlier = span_scores(
        query_blk, key_blk, key_sum, first_span
    )
    value_h = value_blk.reshape(key_h.shape)
    value_sh = value_sum.reshape(key_sh.shape)
    near_prob = jnp.where(causal, jnp.exp(near_score - log_total), 0.0)
    far_prob = jnp.where(earlier, jnp.exp(far_score - log_total), 0.0)
    near_low = near_prob.astype(jnp.bfloat16)
    far_low = far_prob.astype(jnp.bfloat16)
    grad_h = grad_att.reshape(query_h.shape)
    d_value = jnp.einsum("bshij,bsihd->bsjhd", near_low, grad_h, preferred_element_type=jnp.float32)
    d_value_sum = jnp.einsum(
        "bshit,bsihd->bthd", far_low, grad_h, preferred_element_type=jnp.float32
    )
    d_near = jnp.einsum("bsihd,bsjhd->bshij", grad_h, value_h, preferred_element_type=jnp.float32)
    d_far = jnp.einsum("bsihd,bthd->bshit", grad_h, value_sh, preferred_element_type=jnp.float32)
    center = jnp.sum(d_near * near_prob, axis=-1, keepdims=True) + jnp.sum(
        d_far * far_prob, axis=-1, keepdims=True
    )
    d_near_s = (near_prob * (d_near - center)).astype(jnp.bfloat16)
    d_far_s = (far_prob * (d_far - center)).astype(jnp.bfloat16)
    scale_qk = HD ** (-0.5)
    d_query = jnp.einsum("bshij,bsjhd->bsihd", d_near_s, key_h, preferred_element_type=jnp.float32)
    d_query = (
        d_query
        + jnp.einsum("bshit,bthd->bsihd", d_far_s, key_sh, preferred_element_type=jnp.float32)
    ) * scale_qk
    d_key = (
        jnp.einsum("bshij,bsihd->bsjhd", d_near_s, query_h, preferred_element_type=jnp.float32)
        * scale_qk
    )
    d_key_sum = (
        jnp.einsum("bshit,bsihd->bthd", d_far_s, query_h, preferred_element_type=jnp.float32)
        * scale_qk
    )
    return (
        d_query.reshape(query_blk.shape),
        d_key.reshape(query_blk.shape),
        d_value.reshape(query_blk.shape),
        d_key_sum.reshape(key_sum.shape),
        d_value_sum.reshape(key_sum.shape),
    )


def body(
    inputs, lengths, cotangent, w_query, w_key, w_value, w_out, w_up, w_down, gain_attn, gain_mlp
):
    seq_count, slots_dev, model_width = inputs.shape
    spans_dev = slots_dev // SPAN
    first_span = lax.axis_index("seq") * spans_dev
    places = lax.axis_index("seq") * slots_dev + jnp.arange(slots_dev, dtype=jnp.int32)
    valid_mask = (places[None, :] < lengths[:, None]).astype(jnp.float32).reshape(-1, 1)
    seq_group = math.gcd(seq_count, max(1, 512 // slots_dev))
    blocks = seq_count // seq_group

    def split_blocks(array):
        return array.reshape((blocks, seq_group) + array.shape[1:])

    full_query, full_key, full_value, full_out, full_up, full_down, full_gain_a, full_gain_m = (
        lax.all_gather(w_query, ("dp", "seq"), axis=0, tiled=True),
        lax.all_gather(w_key, ("dp", "seq"), axis=0, tiled=True),
        lax.all_gather(w_value, ("dp", "seq"), axis=0, tiled=True),
        lax.all_gather(w_out, ("dp", "seq"), axis=0, tiled=True),
        lax.all_gather(w_up, ("dp", "seq"), axis=0, tiled=True),
        lax.all_gather(w_down, ("dp", "seq"), axis=0, tiled=True),
        lax.all_gather(gain_attn, ("dp", "seq"), axis=0, tiled=True),
        lax.all_gather(gain_mlp, ("dp", "seq"), axis=0, tiled=True),
    )
    flat_in = inputs.reshape(-1, model_width).astype(jnp.float32)
    normal_f, norm_first = jax.vjp(normed, flat_in, full_gain_a.astype(jnp.float32))
    normal_in = normal_f.astype(jnp.bfloat16)
    query = jnp.dot(normal_in, full_query, preferred_element_type=jnp.float32).astype(jnp.bfloat16)
    keys_all = jnp.dot(normal_in, full_key, preferred_element_type=jnp.float32).astype(jnp.bfloat16)
    values_all = jnp.dot(normal_in, full_value, preferred_element_type=jnp.float32).astype(
        jnp.bfloat16
    )
    key_sum = jnp.mean(
        keys_all.reshape(seq_count, spans_dev, SPAN, model_width), axis=2, dtype=jnp.float32
    ).astype(jnp.bfloat16)
    value_sum = jnp.mean(
        values_all.reshape(seq_count, spans_dev, SPAN, model_width), axis=2, dtype=jnp.float32
    ).astype(jnp.bfloat16)
    key_every, value_every = (
        lax.all_gather(key_sum, "seq", axis=1, tiled=True),
        lax.all_gather(value_sum, "seq", axis=1, tiled=True),
    )
    query_b = split_blocks(query.reshape(seq_count, slots_dev, model_width))
    key_b = split_blocks(keys_all.reshape(seq_count, slots_dev, model_width))
    value_b = split_blocks(values_all.reshape(seq_count, slots_dev, model_width))
    key_every_b = split_blocks(key_every)
    value_every_b = split_blocks(value_every)
    attended, log_total = lax.map(
        partial(attend_forward, first_span), (query_b, key_b, value_b, key_every_b, value_every_b)
    )
    attended = attended.reshape(-1, model_width)
    residual_mid = flat_in + jnp.dot(attended, full_out, preferred_element_type=jnp.float32)
    normal_mf, norm_second = jax.vjp(normed, residual_mid, full_gain_m.astype(jnp.float32))
    normal_mid = normal_mf.astype(jnp.bfloat16)
    up_proj = jnp.dot(normal_mid, full_up, preferred_element_type=jnp.float32)
    activated_f, gelu_back = jax.vjp(jax.nn.gelu, up_proj)
    activated = activated_f.astype(jnp.bfloat16)
    result = (
        residual_mid + jnp.dot(activated, full_down, preferred_element_type=jnp.float32)
    ) * valid_mask
    output = result.reshape(seq_count, slots_dev, model_width).astype(jnp.bfloat16)
    full_query, full_key, full_value, full_out, full_up, full_down, full_gain_a, full_gain_m = (
        lax.all_gather(w_query, ("dp", "seq"), axis=0, tiled=True),
        lax.all_gather(w_key, ("dp", "seq"), axis=0, tiled=True),
        lax.all_gather(w_value, ("dp", "seq"), axis=0, tiled=True),
        lax.all_gather(w_out, ("dp", "seq"), axis=0, tiled=True),
        lax.all_gather(w_up, ("dp", "seq"), axis=0, tiled=True),
        lax.all_gather(w_down, ("dp", "seq"), axis=0, tiled=True),
        lax.all_gather(gain_attn, ("dp", "seq"), axis=0, tiled=True),
        lax.all_gather(gain_mlp, ("dp", "seq"), axis=0, tiled=True),
    )
    grad_res = cotangent.reshape(-1, model_width).astype(jnp.float32) * valid_mask
    grad_branch = grad_res.astype(jnp.bfloat16)
    d_down = jnp.einsum("nf,nd->fd", activated, grad_branch, preferred_element_type=jnp.float32)
    d_act = jnp.einsum("nd,fd->nf", grad_branch, full_down, preferred_element_type=jnp.float32)
    d_upper = gelu_back(d_act)[0].astype(jnp.bfloat16)
    d_up = jnp.einsum("nd,nf->df", normal_mid, d_upper, preferred_element_type=jnp.float32)
    d_hn = jnp.einsum("nf,df->nd", d_upper, full_up, preferred_element_type=jnp.float32)
    d_mid_norm, d_gain_m = norm_second(d_hn)
    d_mid = grad_res + d_mid_norm
    d_branch = d_mid.astype(jnp.bfloat16)
    d_out = jnp.einsum("nd,ne->de", attended, d_branch, preferred_element_type=jnp.float32)
    d_att = jnp.einsum("ne,de->nd", d_branch, full_out, preferred_element_type=jnp.float32).astype(
        jnp.bfloat16
    )
    d_att_b = split_blocks(d_att.reshape(seq_count, slots_dev, model_width))
    d_query, d_key, d_value, d_key_sum, d_value_sum = lax.map(
        partial(attend_backward, first_span),
        (query_b, key_b, value_b, key_every_b, value_every_b, log_total, d_att_b),
    )
    d_key_sum = d_key_sum.reshape(seq_count, -1, model_width)
    d_value_sum = d_value_sum.reshape(seq_count, -1, model_width)
    own_key, own_value = (
        lax.psum_scatter(
            d_key_sum.astype(jnp.bfloat16), "seq", scatter_dimension=1, tiled=True
        ).astype(jnp.float32),
        lax.psum_scatter(
            d_value_sum.astype(jnp.bfloat16), "seq", scatter_dimension=1, tiled=True
        ).astype(jnp.float32),
    )
    d_query = d_query.reshape(-1, model_width).astype(jnp.bfloat16)
    d_key = (
        (d_key.reshape(seq_count, spans_dev, SPAN, model_width) + own_key[:, :, None, :] / SPAN)
        .reshape(-1, model_width)
        .astype(jnp.bfloat16)
    )
    d_value = (
        (d_value.reshape(seq_count, spans_dev, SPAN, model_width) + own_value[:, :, None, :] / SPAN)
        .reshape(-1, model_width)
        .astype(jnp.bfloat16)
    )
    d_wquery = jnp.einsum("nd,ne->de", normal_in, d_query, preferred_element_type=jnp.float32)
    d_wkey = jnp.einsum("nd,ne->de", normal_in, d_key, preferred_element_type=jnp.float32)
    d_wvalue = jnp.einsum("nd,ne->de", normal_in, d_value, preferred_element_type=jnp.float32)
    d_normal = jnp.einsum("ne,de->nd", d_query, full_query, preferred_element_type=jnp.float32)
    d_normal = d_normal + jnp.einsum(
        "ne,de->nd", d_key, full_key, preferred_element_type=jnp.float32
    )
    d_normal = d_normal + jnp.einsum(
        "ne,de->nd", d_value, full_value, preferred_element_type=jnp.float32
    )
    d_in_norm, d_gain_a = norm_first(d_normal)
    grad_input = (d_mid + d_in_norm).reshape(seq_count, slots_dev, model_width)
    sent_query, sent_key, sent_value, sent_out, sent_up, sent_down, sent_gain_a, sent_gain_m = (
        lax.psum_scatter(d_wquery, ("dp", "seq"), scatter_dimension=0, tiled=True),
        lax.psum_scatter(d_wkey, ("dp", "seq"), scatter_dimension=0, tiled=True),
        lax.psum_scatter(d_wvalue, ("dp", "seq"), scatter_dimension=0, tiled=True),
        lax.psum_scatter(d_out, ("dp", "seq"), scatter_dimension=0, tiled=True),
        lax.psum_scatter(d_up, ("dp", "seq"), scatter_dimension=0, tiled=True),
        lax.psum_scatter(d_down, ("dp", "seq"), scatter_dimension=0, tiled=True),
        lax.psum_scatter(d_gain_a, ("dp", "seq"), scatter_dimension=0, tiled=True),
        lax.psum_scatter(d_gain_m, ("dp", "seq"), scatter_dimension=0, tiled=True),
    )
    return (
        output,
        grad_input,
        sent_query,
        sent_key,
        sent_value,
        sent_out,
        sent_up,
        sent_down,
        sent_gain_a,
        sent_gain_m,
    )


def solution(mesh):
    placed = (
        P("dp", "seq", None),
        P("dp"),
        P("dp", "seq", None),
        P(("dp", "seq"), None),
        P(("dp", "seq"), None),
        P(("dp", "seq"), None),
        P(("dp", "seq"), None),
        P(("dp", "seq"), None),
        P(("dp", "seq"), None),
        P(("dp", "seq")),
        P(("dp", "seq")),
    )
    return jax.shard_map(
        body,
        mesh=mesh,
        in_specs=placed,
        out_specs=(
            P("dp", "seq", None),
            P("dp", "seq", None),
            P(("dp", "seq"), None),
            P(("dp", "seq"), None),
            P(("dp", "seq"), None),
            P(("dp", "seq"), None),
            P(("dp", "seq"), None),
            P(("dp", "seq"), None),
            P(("dp", "seq")),
            P(("dp", "seq")),
        ),
        check_vma=False,
    )
```

profile of v0, /device:TPU:0, one launch (start us, length us, event | category | flops | bytes accessed | tf_op | source)
XLA Modules:
  0.0 1910.4 jit_solution(12881387140663863526)
XLA Ops:
  10.5 42.0 %all-reduce.5 = (bf16[512]{0:T(512)(128)(2,1)S(1)}, bf16[512]{0:T(512)(128)(2,1)S(1)}) all-reduce(bf16[512]{0:T(512)(128)(2,1)S(1)} %dynamic-update-slice, bf16[512]{0:T(512)(128)(2,1)S(1)} %dynamic-update-slice.1), channel_id=1, replica_groups=mesh['dp'=8,'seq'=4] {'dp','seq'}, use_global_device_ids=true, to_apply=%add | all-reduce | flops 1024 | bytes 4096
  52.5 4.3 fusion.62
  58.1 42.3 %all_gather.37 = bf16[512,512]{1,0:T(8,128)(2,1)S(1)} all-gather(bf16[16,512]{1,0:T(8,128)(2,1)} %param.20), channel_id=1, replica_groups=mesh['dp'=8,'seq'=4] {'dp','seq'}, dimensions={0}, use_global_device_ids=true | all-gather | bytes 540672 | tf_op jit(solution)/shard_map/all_gather | solution.py:129
  100.4 4.5 fusion.60
  107.6 5.3 convolution_convert_fusion.3
  112.9 8.7 copy.291
  121.6 38.0 %all_gather.39 = bf16[512,512]{1,0:T(8,128)(2,1)S(1)} all-gather(bf16[16,512]{1,0:T(8,128)(2,1)S(1)} %copy-done.27), channel_id=1, replica_groups=mesh['dp'=8,'seq'=4] {'dp','seq'}, dimensions={0}, use_global_device_ids=true | all-gather | bytes 540672 | tf_op jit(solution)/shard_map/all_gather | solution.py:128
  159.6 8.3 convolution_convert_fusion.1
  167.9 8.9 copy.293
  176.8 4.3 convert_reduce_fusion.1
  181.1 5.6 all_gather.40
  187.5 4.1 convert_reduce_fusion
  191.7 5.6 all_gather.41
  198.1 39.5 %all_gather.38 = bf16[512,512]{1,0:T(8,128)(2,1)S(1)} all-gather(bf16[16,512]{1,0:T(8,128)(2,1)S(1)} %copy-done.28), channel_id=1, replica_groups=mesh['dp'=8,'seq'=4] {'dp','seq'}, dimensions={0}, use_global_device_ids=true | all-gather | bytes 540672 | tf_op jit(solution)/shard_map/all_gather | solution.py:127
  237.6 5.3 convolution_convert_fusion.2
  242.9 8.7 copy.292
  251.6 131.3 %while.30 = (s32[]{:T(128)}, bf16[12,2,256,512]{3,2,1,0:T(8,128)(2,1)}, f32[12,2,2,8,128,1]{4,3,2,1,5,0:T(8,128)}, bf16[12,2,256,512]{2,3,1,0:T(8,128)(2,1)}, bf...) while((s32[]{:T(128)}, ...), condition=%wide.region_8.9_spmd, body=%wide.region_3.8_spmd.sunk | while | flops 149696528 | bytes 21431460 | solution.py:159
  382.9 38.0 %all_gather.42 = bf16[512,512]{1,0:T(8,128)(2,1)S(1)} all-gather(bf16[16,512]{1,0:T(8,128)(2,1)S(1)} %copy-done.29), channel_id=1, replica_groups=mesh['dp'=8,'seq'=4] {'dp','seq'}, dimensions={0}, use_global_device_ids=true | all-gather | bytes 540672 | tf_op jit(solution)/shard_map/all_gather | solution.py:130
  420.9 10.5 multiply_reduce_fusion.4
  432.8 7.0 fusion.55
  439.8 34.2 %multiply_convert_fusion.2 = (bf16[6144,2048]{1,0:T(8,128)(2,1)}, f32[6144,2048]{1,0:T(8,128)}) fusion(bf16[512,2048]{1,0:T(8,128)(2,1)} %all-gather.3.cloned.1.call-done, f32[6144,512]{1,0:T(8,128)} %get-tuple-element.331, f32[512]{0:T(512)S(1)} %convert_element_type.181, f32[6144]{0:T(1024)S(1)} %fusion.73), kind=kOutput, calls=%fused_computation.104 | convolution fusion | flops 13007585280 | bytes 90204160 | tf_op jit(solution)/shard_map/dot_general | solution.py:166
  474.1 46.7 %fusion.52 = bf16[6144,2048]{1,0:T(8,128)(2,1)} fusion(f32[6144,2048]{1,0:T(8,128)} %get-tuple-element.333, bf16[6144,512]{1,0:T(8,128)(2,1)} %fusion.55, bf16[2048,512]{1,0:T(8,128)(2,1)} %all-gather.5.cloned.1.call-done), kind=kOutput, calls=%fused_computation.103 | convolution fusion | flops 13136560128 | bytes 83886080 | tf_op jit(solution)/shard_map/nd,fd->nf/dot_general | solution.py:186
  520.7 24.2 %multiply_reduce_fusion.2 = (f32[512]{0:T(512)}, f32[6144]{0:T(1024)S(1)}, f32[6144,512]{1,0:T(8,128)}) fusion(f32[6144,512]{1,0:T(8,128)} %get-tuple-element.331, f32[6144]{0:T(1024)S(1)} %fusion.73, f32[512]{0:T(512)S(1)} %convert_element_type.181, bf16[6144,2048]{1,0:T(8,128)(2,1)} %fusion.52, bf16[512,2048]{1,0:T(8,128)(2,1)S(1)} %copy-done.33), kind=kOutput, calls=%fused_computation.131 | convolution fusion | flops 12903770112 | bytes 52482048 | tf_op jit(solution)/shard_map/nf,df->nd/dot_general | solution.py:189
  545.0 11.9 fusion.53
  556.9 6.0 convolution_convert_fusion
  563.3 481.5 %while.31 = (s32[]{:T(128)}, bf16[12,2,256,512]{3,2,1,0:T(8,128)(2,1)}, f32[12,2,256,512]{3,2,1,0:T(8,128)}, f32[12,2,256,512]{3,2,1,0:T(8,128)}, bf16[12,2,8,51...) while((s32[]{:T(128)}, ...), condition=%wide.region_14.15_spmd, body=%wide.region_11.14_spmd.sunk | while | flops 363163648 | bytes 61441868 | solution.py:198
  581.7 3.1 copy.501
  590.4 3.2 copy.500
  621.9 3.1 copy.501
  630.6 3.2 copy.500
  670.7 3.2 copy.500
  702.1 3.1 copy.501
  710.8 3.2 copy.500
  742.2 3.1 copy.501
  750.9 3.2 copy.500
  791.0 3.2 copy.500
  831.1 3.2 copy.500
  871.1 3.2 copy.500
  911.2 3.2 copy.500
  951.4 3.2 copy.500
  991.5 3.2 copy.500
  1031.7 3.2 copy.500
  1046.7 7.1 fusion.64
  1054.6 9.0 fusion.79
  1064.2 10.8 fusion.66
  1077.6 6.4 add_convert_fusion
  1084.0 4.4 fusion.81
  1091.0 6.3 add_convert_fusion.1
  1097.4 4.4 fusion.80
  1101.9 23.2 %fusion.74 = f32[512,2048]{1,0:T(8,128)} fusion(bf16[6144,2048]{1,0:T(8,128)(2,1)} %fusion.52, f32[6144,512]{1,0:T(8,128)} %get-tuple-element.331, f32[512]{0:T(512)S(1)} %convert_element_type.181, f32[6144]{0:T(1024)S(1)} %fusion.73), kind=kOutput, calls=%fused_computation.161 | convolution fusion | flops 12894339072 | bytes 41969664 | tf_op jit(solution)/shard_map/nd,nf->df/dot_general | solution.py:188
  1125.4 21.2 %fusion.82 = f32[2048,512]{1,0:T(8,128)} fusion(bf16[6144,2048]{1,0:T(8,128)(2,1)} %get-tuple-element.332, bf16[6144,512]{1,0:T(8,128)(2,1)} %fusion.55), kind=kOutput, calls=%fused_computation.169 | convolution fusion | flops 12884901888 | bytes 35651584 | tf_op jit(solution)/shard_map/nf,nd->fd/dot_general | solution.py:185
  1146.7 21.6 %multiply_convert_fusion.3 = bf16[6144,512]{1,0:T(8,128)(2,1)} fusion(f32[6144,512]{1,0:T(8,128)} %get-tuple-element.331, bf16[6144,2048]{1,0:T(8,128)(2,1)} %get-tuple-element.332, bf16[2048,512]{1,0:T(8,128)(2,1)S(1)} %copy-done.32, f32[6144]{0:T(1024)S(1)} %bitcast.273), kind=kOutput, calls=%fused_computation.136 | convolution fusion | flops 12894339072 | bytes 46161920 | tf_op jit(solution)/shard_map/dot_general | solution.py:170
  1168.3 9.6 fusion.77
  1177.9 9.1 fusion.57
  1187.0 9.2 fusion.56
  1196.1 9.4 fusion.78
  1205.5 20.2 %fusion.61 = (f32[512]{0:T(512)S(1)}, f32[6144]{0:T(1024)S(1)}, f32[6144,512]{1,0:T(8,128)}) fusion(bf16[24,256,512]{2,1,0:T(8,128)(2,1)} %param.15, f32[6144]{0:T(1024)S(1)} %copy-done.15, f32[512]{0:T(512)S(1)} %copy-done.26, bf16[6144,512]{1,0:T(8,128)(2,1)} %fusion.56, bf16[512,512]{1,0:T(8,128)(2,1)S(1)} %copy-done.9, f32[6144,512]{1,0:T(8,128)} %fusion.77, ...), kind=kOutput, calls=%fused_computation.126 | convolution fusion | flops 3249530368 | bytes 50909184 | tf_op jit(solution)/shard_map/ne,de->nd/dot_general | solution.py:230
  1225.8 37.0 %all-reduce.4 = (f32[512]{0:T(512)S(1)}, f32[512]{0:T(512)S(1)}) all-reduce(f32[512]{0:T(512)S(1)} %get-tuple-element.258, f32[512]{0:T(512)S(1)} %copy-done.30), channel_id=10, replica_groups=mesh['dp'=8,'seq'=4] {'dp','seq'}, use_global_device_ids=true, to_apply=%region_25.26.clone | all-reduce | flops 1024 | bytes 8192
  1263.9 16.3 fusion.54
  1280.2 76.8 %reduce-scatter.19.cloned.1.call-done = f32[16,512]{1,0:T(8,128)} async-done(((f32[512,512]{1,0:T(8,128)}), f32[16,512]{1,0:T(8,128)}) %reduce-scatter.19.cloned.1.call-update) | async-done | bytes 32784 | tf_op jit(solution)/shard_map/reduce_scatter | solution.py:239
  1357.0 133.7 %reduce-scatter.17.cloned.1.call-done = f32[16,512]{1,0:T(8,128)} async-done(((f32[512,512]{1,0:T(8,128)}), f32[16,512]{1,0:T(8,128)}) %reduce-scatter.17.cloned.1.call-update) | async-done | bytes 32784 | tf_op jit(solution)/shard_map/reduce_scatter | solution.py:238
  1490.7 133.6 %reduce-scatter.15.cloned.1.call-done = f32[16,512]{1,0:T(8,128)} async-done(((f32[512,512]{1,0:T(8,128)}), f32[16,512]{1,0:T(8,128)}) %reduce-scatter.15.cloned.1.call-update) | async-done | bytes 32784 | tf_op jit(solution)/shard_map/reduce_scatter | solution.py:237
  1624.3 139.6 %reduce-scatter.21.cloned.1.call-done = f32[16,2048]{1,0:T(8,128)} async-done(((f32[512,2048]{1,0:T(8,128)}), f32[16,2048]{1,0:T(8,128)}) %reduce-scatter.21.cloned.1.call-update) | async-done | bytes 131088 | tf_op jit(solution)/shard_map/reduce_scatter | solution.py:240
  1763.9 139.5 %reduce-scatter.23.cloned.1.call-done = f32[64,512]{1,0:T(8,128)} async-done(((f32[2048,512]{1,0:T(8,128)}), f32[64,512]{1,0:T(8,128)}) %reduce-scatter.23.cloned.1.call-update) | async-done | bytes 131088 | tf_op jit(solution)/shard_map/reduce_scatter | solution.py:241
  (1044 shorter events, 578.5 us)
Async XLA Ops:
  7.2 432.7 %all-gather.3.cloned.1.call-start = ((), (), s32[]{:S(2)}) async-start(), calls=%async_computation.8 | async-start | bytes 2162688 | tf_op jit(solution)/shard_map/all_gather | solution.py:131
  7.9 466.1 %all-gather.5.cloned.1.call-start = ((), (), s32[]{:S(2)}) async-start(), calls=%async_computation.9 | async-start | bytes 2162688 | tf_op jit(solution)/shard_map/all_gather | solution.py:132
  8.7 1066.4 %reduce-scatter.11.cloned.1.call-start = ((), (), s32[]{:S(2)}) async-start(), calls=%async_computation.11 | async-start | bytes 245760 | tf_op jit(solution)/shard_map/reduce_scatter | solution.py:208
  52.5 60.4 %copy-start.25 = (f32[512]{0:T(512)}, f32[512]{0:T(512)S(1)}, u32[]{:S(2)}) copy-start(f32[512]{0:T(512)S(1)} %convert_element_type.170) | copy-start | bytes 6148
  58.1 42.3 %copy-start.14 = (f32[6144]{0:T(1024)}, f32[6144]{0:T(1024)S(1)}, u32[]{:S(2)}) copy-start(f32[6144]{0:T(1024)S(1)} %rsqrt.23) | copy-start | bytes 73732
  100.4 12.5 copy-start.8
  107.6 14.0 copy-start.27
  167.9 30.1 %copy-start.28 = (bf16[16,512]{1,0:T(8,128)(2,1)S(1)}, bf16[16,512]{1,0:T(8,128)(2,1)}, u32[]{:S(2)}) copy-start(bf16[16,512]{1,0:T(8,128)(2,1)} %param.18) | copy-start | bytes 49156
  167.9 69.7 %slice-start.4 = ((s8[6291456]{0:T(1024)(128)(4,1)}), s8[2097152]{0:T(1024)(128)(4,1)S(1)}, s32[]{:S(2)}) async-start(s8[6291456]{0:T(1024)(128)(4,1)} %bitcast.259), calls=%async_computation.22 | async-start | bytes 4194304
  176.8 60.8 %slice-start.5 = ((s8[6291456]{0:T(1024)(128)(4,1)}), s8[4194304]{0:T(1024)(128)(4,1)S(1)}, s32[]{:S(2)}) async-start(s8[6291456]{0:T(1024)(128)(4,1)} %bitcast.259), calls=%async_computation.23 | async-start | bytes 8388608
  251.6 131.3 %copy-start.29 = (bf16[16,512]{1,0:T(8,128)(2,1)S(1)}, bf16[16,512]{1,0:T(8,128)(2,1)}, u32[]{:S(2)}) copy-start(bf16[16,512]{1,0:T(8,128)(2,1)} %param.21) | copy-start | bytes 49156
  474.1 46.7 %copy-start.33 = (bf16[512,2048]{1,0:T(8,128)(2,1)S(1)}, bf16[512,2048]{1,0:T(8,128)(2,1)}, u32[]{:S(2)}) copy-start(bf16[512,2048]{1,0:T(8,128)(2,1)} %all-gather.3.cloned.1.call-done) | copy-start | bytes 6291460
  520.7 24.2 %copy-start.17 = (f32[6144]{0:T(1024)S(1)}, f32[6144]{0:T(1024)}, u32[]{:S(2)}) copy-start(f32[6144]{0:T(1024)} %copy-done.16) | copy-start | bytes 73732
  520.7 24.2 %copy-start.21 = (f32[3,2,8,128]{3,1,2,0:T(2,128)S(1)}, f32[3,2,8,128]{3,1,2,0:T(2,128)}, u32[]{:S(2)}) copy-start(f32[3,2,8,128]{3,1,2,0:T(2,128)} %copy-done.20) | copy-start | bytes 73732
  545.0 11.9 copy-start.7
  563.3 483.3 %copy-start.24 = (f32[24,256]{1,0:T(8,128)S(1)}, f32[24,256]{1,0:T(8,128)}, u32[]{:S(2)}) copy-start(f32[24,256]{1,0:T(8,128)} %get-tuple-element.328) | copy-start | bytes 73732
  563.3 483.3 %copy-start.26 = (f32[512]{0:T(512)S(1)}, f32[512]{0:T(512)}, u32[]{:S(2)}) copy-start(f32[512]{0:T(512)} %copy-done.25) | copy-start | bytes 6148
  564.7 13.7 copy-start.3
  590.4 11.9 copy-start.4
  590.4 12.3 copy-start.1
  604.9 13.7 copy-start.3
  630.6 11.8 copy-start.4
  630.6 12.2 copy-start.1
  645.0 13.7 copy-start.3
  670.7 11.9 copy-start.4
  670.7 12.2 copy-start.1
  685.1 13.7 copy-start.3
  710.8 11.8 copy-start.4
  710.8 12.2 copy-start.1
  725.2 13.7 copy-start.3
  750.9 11.8 copy-start.4
  750.9 12.2 copy-start.1
  765.3 13.7 copy-start.3
  791.0 11.8 copy-start.4
  791.0 12.2 copy-start.1
  805.4 13.7 copy-start.3
  831.1 12.1 copy-start.1
  845.4 13.7 copy-start.3
  871.1 11.9 copy-start.4
  871.1 12.2 copy-start.1
  885.5 13.7 copy-start.3
  911.2 11.9 copy-start.4
  911.2 12.3 copy-start.1
  925.7 13.7 copy-start.3
  951.4 11.8 copy-start.4
  951.4 12.2 copy-start.1
  965.8 13.7 copy-start.3
  991.5 11.8 copy-start.4
  991.5 12.2 copy-start.1
  1005.9 13.7 copy-start.3
  1031.6 11.9 copy-start.4
  1031.7 12.2 copy-start.1
  1046.6 41.9 %reduce-scatter.9.cloned.1.call-start = ((), (), s32[]{:S(2)}) async-start(), calls=%async_computation.10 | async-start | bytes 245760 | tf_op jit(solution)/shard_map/reduce_scatter | solution.py:205
  1054.6 225.6 %reduce-scatter.13.cloned.1.call-start = ((), (), s32[]{:S(2)}) async-start(), calls=%async_computation.12 | async-start | bytes 1081344 | tf_op jit(solution)/shard_map/reduce_scatter | solution.py:236
  1063.7 293.3 %reduce-scatter.19.cloned.1.call-start = ((), (), s32[]{:S(2)}) async-start(), calls=%async_computation.15 | async-start | bytes 1081344 | tf_op jit(solution)/shard_map/reduce_scatter | solution.py:239
  1075.0 415.7 %reduce-scatter.17.cloned.1.call-start = ((), (), s32[]{:S(2)}) async-start(), calls=%async_computation.14 | async-start | bytes 1081344 | tf_op jit(solution)/shard_map/reduce_scatter | solution.py:238
  1088.4 535.8 %reduce-scatter.15.cloned.1.call-start = ((), (), s32[]{:S(2)}) async-start(), calls=%async_computation.13 | async-start | bytes 1081344 | tf_op jit(solution)/shard_map/reduce_scatter | solution.py:237
  1101.8 662.0 %reduce-scatter.21.cloned.1.call-start = ((), (), s32[]{:S(2)}) async-start(), calls=%async_computation.16 | async-start | bytes 4325376 | tf_op jit(solution)/shard_map/reduce_scatter | solution.py:240
  1125.1 778.2 %reduce-scatter.23.cloned.1.call-start = ((), (), s32[]{:S(2)}) async-start(), calls=%async_computation.17 | async-start | bytes 4325376 | tf_op jit(solution)/shard_map/reduce_scatter | solution.py:241
  1125.4 21.3 %copy-start.22 = (f32[3,2,8,128]{3,1,2,0:T(2,128)S(1)}, f32[3,2,8,128]{3,1,2,0:T(2,128)}, u32[]{:S(2)}) copy-start(f32[3,2,8,128]{3,1,2,0:T(2,128)} %copy-done.20) | copy-start | bytes 73732
  1125.4 21.3 %copy-start.32 = (bf16[2048,512]{1,0:T(8,128)(2,1)S(1)}, bf16[2048,512]{1,0:T(8,128)(2,1)}, u32[]{:S(2)}) copy-start(bf16[2048,512]{1,0:T(8,128)(2,1)} %all-gather.5.cloned.1.call-done) | copy-start | bytes 6291460
  1146.7 21.6 %copy-start.13 = (bf16[512,512]{1,0:T(8,128)(2,1)S(1)}, bf16[512,512]{1,0:T(8,128)(2,1)}, u32[]{:S(2)}) copy-start(bf16[512,512]{1,0:T(8,128)(2,1)} %copy-done.12) | copy-start | bytes 1572868
  1205.5 20.3 %copy-start.30 = (f32[512]{0:T(512)S(1)}, f32[512]{0:T(512)}, u32[]{:S(2)}) copy-start(f32[512]{0:T(512)} %get-tuple-element.256) | copy-start | bytes 6148
  1205.5 58.4 %copy-start.19 = (f32[3,2,8,128]{3,1,2,0:T(2,128)S(1)}, f32[3,2,8,128]{3,1,2,0:T(2,128)}, u32[]{:S(2)}) copy-start(f32[3,2,8,128]{3,1,2,0:T(2,128)} %copy-done.18) | copy-start | bytes 73732
  (30 other events, 247.8 us)
Sparse Core Ops, SparseCore 0:
  10.9 59.1 all-gather.2
  72.9 55.7 all-gather.4
  1046.7 17.1 reduce-scatter.10
  1066.2 19.7 reduce-scatter.8
  1088.6 134.7 reduce-scatter.12
  1226.2 130.7 reduce-scatter.18
  1359.8 130.8 reduce-scatter.16
  1493.6 130.6 reduce-scatter.14
  1627.1 136.7 reduce-scatter.20
  1766.6 136.7 reduce-scatter.22
where the time goes:
time: 1930 us; the launch traced here: 1910 us
  waiting for transfers between devices  625 us (32%)
  matrix products  462 us (24%)
  local copies, waits for them, and re-layouts  441 us (23%)
  blocking collectives  248 us (13%)
  other arithmetic  115 us (6%)
    dynamic_update_slice x108, local copies, waits for them, and re-layouts, body(): lax.map(partial(attend_backward, first_span), (query_b, key_b, value_b, k...  197 us
    reduce_scatter x1, waiting for transfers between devices, body(): lax.psum_scatter(d_up, ('dp', 'seq'), scatter_dimension=0, tiled=True)  140 us
    reduce_scatter x1, waiting for transfers between devices, body(): lax.psum_scatter(d_down, ('dp', 'seq'), scatter_dimension=0, tiled=True)  139 us
    reduce_scatter x1, waiting for transfers between devices, body(): lax.psum_scatter(d_wvalue, ('dp', 'seq'), scatter_dimension=0, tiled=True)  134 us
    reduce_scatter x1, waiting for transfers between devices, body(): lax.psum_scatter(d_wkey, ('dp', 'seq'), scatter_dimension=0, tiled=True)  134 us
    dynamic_slice x120, local copies, waits for them, and re-layouts, body(): lax.map(partial(attend_forward, first_span), (query_b, key_b, value_b, ke...  120 us
    unnamed x2, blocking collectives  79 us
    reduce_scatter x1, waiting for transfers between devices, body(): lax.psum_scatter(d_out, ('dp', 'seq'), scatter_dimension=0, tiled=True)  76.8 us
  transfers between devices with their start and end apart: 10, of which 5 were waited for; matrix products, arithmetic and copies ran while one was open for 23% of the time, Pallas kernels for 0%

commit v1 on v0

--- a/solution.py
+++ b/solution.py
@@ -126,7 +126,12 @@
     full_query, full_key, full_value, full_out, full_up, full_down, full_gain_a, full_gain_m = (
         lax.all_gather(w_query, ("dp", "seq"), axis=0, tiled=True),
         lax.all_gather(w_key, ("dp", "seq"), axis=0, tiled=True),
-        lax.all_gather(w_value, ("dp", "seq"), axis=0, tiled=True),
+        jnp.concatenate(
+            lax.all_to_all(
+                jnp.stack([w_value] * lax.axis_size(("dp", "seq"))), ("dp", "seq"), 0, 0
+            ),
+            axis=0,
+        ),
         lax.all_gather(w_out, ("dp", "seq"), axis=0, tiled=True),
         lax.all_gather(w_up, ("dp", "seq"), axis=0, tiled=True),
         lax.all_gather(w_down, ("dp", "seq"), axis=0, tiled=True),

time: 1930 us -> 1910 us (0.990)
  waiting for transfers between devices: 625 us -> 589 us
    reduce_scatter x1, waiting for transfers between devices: 76.8 us -> 37.8 us  [body(): lax.psum_scatter(d_out, ('dp', 'seq'), scatter_dimension=0, tiled=True)]
  transfers between devices with their start and end apart: 10 -> 11, of which waited for: 5 -> 6; matrix products, arithmetic and copies ran while one was open for 23% -> 23% of each run, Pallas kernels for 0% -> 0%
where the time goes in v1:
time: 1910 us; the launch traced here: 1890 us
  waiting for transfers between devices  589 us (31%)
  matrix products  464 us (24%)
  local copies, waits for them, and re-layouts  444 us (23%)
  blocking collectives  254 us (13%)
  other arithmetic  111 us (6%)
    dynamic_update_slice x108, local copies, waits for them, and re-layouts, body(): lax.map(partial(attend_backward, first_span), (query_b, key_b, value_b, k...  197 us
    reduce_scatter x1, waiting for transfers between devices, body(): lax.psum_scatter(d_down, ('dp', 'seq'), scatter_dimension=0, tiled=True)  140 us
    reduce_scatter x1, waiting for transfers between devices, body(): lax.psum_scatter(d_up, ('dp', 'seq'), scatter_dimension=0, tiled=True)  140 us
    reduce_scatter x1, waiting for transfers between devices, body(): lax.psum_scatter(d_wkey, ('dp', 'seq'), scatter_dimension=0, tiled=True)  134 us
    reduce_scatter x1, waiting for transfers between devices, body(): lax.psum_scatter(d_wvalue, ('dp', 'seq'), scatter_dimension=0, tiled=True)  134 us
    dynamic_slice x120, local copies, waits for them, and re-layouts, body(): lax.map(partial(attend_forward, first_span), (query_b, key_b, value_b, ke...  120 us
    unnamed x2, blocking collectives  77.8 us
    dot_general x1, matrix products, body(): jnp.einsum('nd,fd->nf', grad_branch, full_down, preferred_element_type=jn...  46.7 us
  transfers between devices with their start and end apart: 11, of which 6 were waited for; matrix products, arithmetic and copies ran while one was open for 23% of the time, Pallas kernels for 0%

profile of v1, /device:TPU:0, one launch (start us, length us, event | category | flops | bytes accessed | tf_op | source)
XLA Modules:
  0.0 1888.2 jit_solution(4030622350752634007)
XLA Ops:
  9.5 7.3 all-to-all-start
  19.3 40.8 %all-reduce.5 = (bf16[512]{0:T(512)(128)(2,1)S(1)}, bf16[512]{0:T(512)(128)(2,1)S(1)}) all-reduce(bf16[512]{0:T(512)(128)(2,1)S(1)} %dynamic-update-slice, bf16[512]{0:T(512)(128)(2,1)S(1)} %dynamic-update-slice.1), channel_id=1, replica_groups=mesh['dp'=8,'seq'=4] {'dp','seq'}, use_global_device_ids=true, to_apply=%add | all-reduce | flops 1024 | bytes 4096
  60.1 4.1 fusion.62
  64.9 42.3 %all_gather.37 = bf16[512,512]{1,0:T(8,128)(2,1)S(1)} all-gather(bf16[16,512]{1,0:T(8,128)(2,1)} %param.19), channel_id=1, replica_groups=mesh['dp'=8,'seq'=4] {'dp','seq'}, dimensions={0}, use_global_device_ids=true | all-gather | bytes 540672 | tf_op jit(solution)/shard_map/all_gather | solution.py:128
  107.2 4.5 fusion.60
  111.7 3.6 convolution_convert_fusion.1
  119.3 38.1 %all_gather.36 = bf16[512,512]{1,0:T(8,128)(2,1)S(1)} all-gather(bf16[16,512]{1,0:T(8,128)(2,1)S(1)} %copy-done.23), channel_id=1, replica_groups=mesh['dp'=8,'seq'=4] {'dp','seq'}, dimensions={0}, use_global_device_ids=true | all-gather | bytes 540672 | tf_op jit(solution)/shard_map/all_gather | solution.py:127
  158.3 5.3 convolution_convert_fusion.2
  164.2 7.0 fusion.55
  171.4 8.7 copy.293
  180.1 5.7 all_gather.38
  186.5 8.7 copy.292
  195.2 42.3 %all_gather.40 = bf16[512,512]{1,0:T(8,128)(2,1)} all-gather(bf16[16,512]{1,0:T(8,128)(2,1)S(1)} %copy-done.24), channel_id=1, replica_groups=mesh['dp'=8,'seq'=4] {'dp','seq'}, dimensions={0}, use_global_device_ids=true | all-gather | bytes 540672 | tf_op jit(solution)/shard_map/all_gather | solution.py:135
  237.5 7.1 fusion.64
  244.6 8.1 convolution_convert_fusion.3
  252.7 8.7 copy.291
  261.4 4.1 convert_reduce_fusion
  265.6 5.6 all_gather.39
  271.9 131.3 %while.30 = (s32[]{:T(128)}, bf16[12,2,256,512]{3,2,1,0:T(8,128)(2,1)}, f32[12,2,2,8,128,1]{4,3,2,1,5,0:T(8,128)}, bf16[12,2,256,512]{2,3,1,0:T(8,128)(2,1)}, bf...) while((s32[]{:T(128)}, ...), condition=%wide.region_8.9_spmd, body=%wide.region_3.8_spmd.sunk | while | flops 149696528 | bytes 21431460 | solution.py:164
  403.2 13.4 multiply_reduce_fusion.4
  417.3 34.4 %multiply_convert_fusion.2 = (bf16[6144,2048]{1,0:T(8,128)(2,1)}, f32[6144,2048]{1,0:T(8,128)}) fusion(bf16[512,2048]{1,0:T(8,128)(2,1)} %all-gather.3.cloned.1.call-done, f32[6144,512]{1,0:T(8,128)} %get-tuple-element.331, f32[512]{0:T(512)S(1)} %convert_element_type.185, f32[6144]{0:T(1024)S(1)} %fusion.73), kind=kOutput, calls=%fused_computation.104 | convolution fusion | flops 13007585280 | bytes 90204160 | tf_op jit(solution)/shard_map/dot_general | solution.py:171
  451.7 46.7 %fusion.52 = bf16[6144,2048]{1,0:T(8,128)(2,1)} fusion(f32[6144,2048]{1,0:T(8,128)} %get-tuple-element.333, bf16[6144,512]{1,0:T(8,128)(2,1)} %fusion.55, bf16[2048,512]{1,0:T(8,128)(2,1)} %all-gather.5.cloned.1.call-done), kind=kOutput, calls=%fused_computation.103 | convolution fusion | flops 13136560128 | bytes 83886080 | tf_op jit(solution)/shard_map/nd,fd->nf/dot_general | solution.py:191
  498.5 24.2 %multiply_reduce_fusion.2 = (f32[512]{0:T(512)}, f32[6144]{0:T(1024)S(1)}, f32[6144,512]{1,0:T(8,128)}) fusion(f32[6144,512]{1,0:T(8,128)} %get-tuple-element.331, f32[6144]{0:T(1024)S(1)} %fusion.73, f32[512]{0:T(512)S(1)} %convert_element_type.185, bf16[6144,2048]{1,0:T(8,128)(2,1)} %fusion.52, bf16[512,2048]{1,0:T(8,128)(2,1)S(1)} %copy-done.28), kind=kOutput, calls=%fused_computation.131 | convolution fusion | flops 12903770112 | bytes 52482048 | tf_op jit(solution)/shard_map/nf,df->nd/dot_general | solution.py:194
  522.7 11.9 fusion.53
  534.7 6.0 convolution_convert_fusion
  541.1 482.0 %while.31 = (s32[]{:T(128)}, bf16[12,2,256,512]{3,2,1,0:T(8,128)(2,1)}, f32[12,2,256,512]{3,2,1,0:T(8,128)}, f32[12,2,256,512]{3,2,1,0:T(8,128)}, bf16[12,2,8,51...) while((s32[]{:T(128)}, ...), condition=%wide.region_14.15_spmd, body=%wide.region_11.14_spmd.sunk | while | flops 363163648 | bytes 61441868 | solution.py:203
  559.5 3.2 copy.501
  568.2 3.2 copy.500
  599.7 3.2 copy.501
  608.4 3.2 copy.500
  648.6 3.2 copy.500
  680.0 3.2 copy.501
  688.7 3.2 copy.500
  728.9 3.2 copy.500
  769.0 3.2 copy.500
  809.2 3.2 copy.500
  840.6 3.2 copy.501
  849.3 3.2 copy.500
  889.5 3.2 copy.500
  929.6 3.2 copy.500
  969.8 3.2 copy.500
  1009.9 3.2 copy.500
  1026.6 9.1 fusion.79
  1036.2 10.9 fusion.66
  1049.7 6.3 add_convert_fusion
  1056.1 4.4 fusion.81
  1065.4 6.3 add_convert_fusion.1
  1071.8 4.4 fusion.80
  1076.3 23.1 %fusion.74 = f32[512,2048]{1,0:T(8,128)} fusion(bf16[6144,2048]{1,0:T(8,128)(2,1)} %fusion.52, f32[6144,512]{1,0:T(8,128)} %get-tuple-element.331, f32[512]{0:T(512)S(1)} %convert_element_type.185, f32[6144]{0:T(1024)S(1)} %fusion.73), kind=kOutput, calls=%fused_computation.161 | convolution fusion | flops 12894339072 | bytes 41969664 | tf_op jit(solution)/shard_map/nd,nf->df/dot_general | solution.py:193
  1099.5 42.1 %all_gather.44 = bf16[512,512]{1,0:T(8,128)(2,1)S(1)} all-gather(bf16[16,512]{1,0:T(8,128)(2,1)S(1)} %copy-done.22), channel_id=1, replica_groups=mesh['dp'=8,'seq'=4] {'dp','seq'}, dimensions={0}, use_global_device_ids=true | all-gather | bytes 540672 | tf_op jit(solution)/shard_map/all_gather | solution.py:181
  1141.6 21.2 %fusion.82 = f32[2048,512]{1,0:T(8,128)} fusion(bf16[6144,2048]{1,0:T(8,128)(2,1)} %get-tuple-element.332, bf16[6144,512]{1,0:T(8,128)(2,1)} %fusion.55), kind=kOutput, calls=%fused_computation.169 | convolution fusion | flops 12884901888 | bytes 35651584 | tf_op jit(solution)/shard_map/nf,nd->fd/dot_general | solution.py:190
  1162.9 21.6 %multiply_convert_fusion.3 = bf16[6144,512]{1,0:T(8,128)(2,1)} fusion(f32[6144,512]{1,0:T(8,128)} %get-tuple-element.331, bf16[6144,2048]{1,0:T(8,128)(2,1)} %get-tuple-element.332, bf16[2048,512]{1,0:T(8,128)(2,1)S(1)} %copy-done.27, f32[6144]{0:T(1024)S(1)} %bitcast.274), kind=kOutput, calls=%fused_computation.136 | convolution fusion | flops 12894339072 | bytes 46161920 | tf_op jit(solution)/shard_map/dot_general | solution.py:175
  1184.5 9.6 fusion.77
  1194.1 9.1 fusion.57
  1203.2 9.2 fusion.56
  1212.4 9.3 fusion.78
  1221.7 20.3 %fusion.61 = (f32[512]{0:T(512)S(1)}, f32[6144]{0:T(1024)S(1)}, f32[6144,512]{1,0:T(8,128)}) fusion(bf16[24,256,512]{2,1,0:T(8,128)(2,1)} %param.15, f32[6144]{0:T(1024)S(1)} %copy-done.12, f32[512]{0:T(512)S(1)} %copy-done.21, bf16[6144,512]{1,0:T(8,128)(2,1)} %fusion.56, bf16[512,512]{1,0:T(8,128)(2,1)S(1)} %all_gather.44, f32[6144,512]{1,0:T(8,128)} %fusion.77, ...), kind=kOutput, calls=%fused_computation.126 | convolution fusion | flops 3249530368 | bytes 50909184 | tf_op jit(solution)/shard_map/ne,de->nd/dot_general | solution.py:235
  1242.0 37.0 %all-reduce.4 = (f32[512]{0:T(512)S(1)}, f32[512]{0:T(512)S(1)}) all-reduce(f32[512]{0:T(512)S(1)} %get-tuple-element.258, f32[512]{0:T(512)S(1)} %copy-done.25), channel_id=10, replica_groups=mesh['dp'=8,'seq'=4] {'dp','seq'}, use_global_device_ids=true, to_apply=%region_25.26.clone | all-reduce | flops 1024 | bytes 8192
  1280.1 16.3 fusion.54
  1296.4 37.8 %reduce-scatter.19.cloned.1.call-done = f32[16,512]{1,0:T(8,128)} async-done(((f32[512,512]{1,0:T(8,128)}), f32[16,512]{1,0:T(8,128)}) %reduce-scatter.19.cloned.1.call-update) | async-done | bytes 32784 | tf_op jit(solution)/shard_map/reduce_scatter | solution.py:244
  1334.2 133.6 %reduce-scatter.17.cloned.1.call-done = f32[16,512]{1,0:T(8,128)} async-done(((f32[512,512]{1,0:T(8,128)}), f32[16,512]{1,0:T(8,128)}) %reduce-scatter.17.cloned.1.call-update) | async-done | bytes 32784 | tf_op jit(solution)/shard_map/reduce_scatter | solution.py:243
  1467.8 133.6 %reduce-scatter.15.cloned.1.call-done = f32[16,512]{1,0:T(8,128)} async-done(((f32[512,512]{1,0:T(8,128)}), f32[16,512]{1,0:T(8,128)}) %reduce-scatter.15.cloned.1.call-update) | async-done | bytes 32784 | tf_op jit(solution)/shard_map/reduce_scatter | solution.py:242
  1601.4 139.8 %reduce-scatter.21.cloned.1.call-done = f32[16,2048]{1,0:T(8,128)} async-done(((f32[512,2048]{1,0:T(8,128)}), f32[16,2048]{1,0:T(8,128)}) %reduce-scatter.21.cloned.1.call-update) | async-done | bytes 131088 | tf_op jit(solution)/shard_map/reduce_scatter | solution.py:245
  1741.2 139.9 %reduce-scatter.23.cloned.1.call-done = f32[64,512]{1,0:T(8,128)} async-done(((f32[2048,512]{1,0:T(8,128)}), f32[64,512]{1,0:T(8,128)}) %reduce-scatter.23.cloned.1.call-update) | async-done | bytes 131088 | tf_op jit(solution)/shard_map/reduce_scatter | solution.py:246
  (1032 shorter events, 584.7 us)
Async XLA Ops:
  7.2 410.1 %all-gather.3.cloned.1.call-start = ((), (), s32[]{:S(2)}) async-start(), calls=%async_computation.9 | async-start | bytes 2162688 | tf_op jit(solution)/shard_map/all_gather | solution.py:136
  9.5 235.2 %all-to-all-start = ((bf16[32,16,512]{2,1,0:T(8,128)(2,1)}), bf16[32,16,512]{2,1,0:T(8,128)(2,1)S(1)}, u32[]{:S(2)}, u32[]{:S(2)}) async-start(bf16[32,16,512]{2,1,0:T(8,128)(2,1)} %stack.2), calls=%async_computation | async-start | bytes 1048576 | tf_op jit(solution)/shard_map/all_to_all | solution.py:130
  16.8 434.9 %all-gather.5.cloned.1.call-start = ((), (), s32[]{:S(2)}) async-start(), calls=%async_computation.10 | async-start | bytes 2162688 | tf_op jit(solution)/shard_map/all_gather | solution.py:137
  17.5 1029.7 %reduce-scatter.11.cloned.1.call-start = ((), (), s32[]{:S(2)}) async-start(), calls=%async_computation.12 | async-start | bytes 245760 | tf_op jit(solution)/shard_map/reduce_scatter | solution.py:213
  60.1 177.4 %copy-start.20 = (f32[512]{0:T(512)}, f32[512]{0:T(512)S(1)}, u32[]{:S(2)}) copy-start(f32[512]{0:T(512)S(1)} %convert_element_type.172) | copy-start | bytes 6148
  64.9 42.3 %copy-start.11 = (f32[6144]{0:T(1024)}, f32[6144]{0:T(1024)S(1)}, u32[]{:S(2)}) copy-start(f32[6144]{0:T(1024)S(1)} %rsqrt.24) | copy-start | bytes 73732
  117.9 45.6 %copy-start.26 = (s32[24]{0:T(128)S(1)}, s32[24]{0:T(128)}, u32[]{:S(2)}) copy-start(s32[24]{0:T(128)} %param.16) | copy-start | bytes 292
  171.4 23.8 %copy-start.24 = (bf16[16,512]{1,0:T(8,128)(2,1)S(1)}, bf16[16,512]{1,0:T(8,128)(2,1)}, u32[]{:S(2)}) copy-start(bf16[16,512]{1,0:T(8,128)(2,1)} %param.21) | copy-start | bytes 49156
  451.7 46.7 %copy-start.28 = (bf16[512,2048]{1,0:T(8,128)(2,1)S(1)}, bf16[512,2048]{1,0:T(8,128)(2,1)}, u32[]{:S(2)}) copy-start(bf16[512,2048]{1,0:T(8,128)(2,1)} %all-gather.3.cloned.1.call-done) | copy-start | bytes 6291460
  498.5 24.2 %copy-start.14 = (f32[6144]{0:T(1024)S(1)}, f32[6144]{0:T(1024)}, u32[]{:S(2)}) copy-start(f32[6144]{0:T(1024)} %copy-done.13) | copy-start | bytes 73732
  498.5 24.3 %copy-start.18 = (f32[3,2,8,128]{3,1,2,0:T(2,128)S(1)}, f32[3,2,8,128]{3,1,2,0:T(2,128)}, u32[]{:S(2)}) copy-start(f32[3,2,8,128]{3,1,2,0:T(2,128)} %copy-done.17) | copy-start | bytes 73732
  522.7 11.9 copy-start.6
  542.5 13.7 copy-start.3
  568.2 11.9 copy-start.4
  568.2 12.3 copy-start.1
  582.7 13.7 copy-start.3
  608.4 11.9 copy-start.4
  608.4 12.2 copy-start.1
  622.9 13.7 copy-start.3
  626.2 10.4 copy-start
  648.6 11.8 copy-start.4
  648.6 12.2 copy-start.1
  663.0 13.7 copy-start.3
  688.7 11.8 copy-start.4
  688.7 12.2 copy-start.1
  703.1 13.7 copy-start.3
  706.5 10.4 copy-start
  728.9 11.9 copy-start.4
  728.9 12.2 copy-start.1
  743.3 13.7 copy-start.3
  769.0 11.9 copy-start.4
  769.0 12.2 copy-start.1
  783.5 13.7 copy-start.3
  809.2 11.8 copy-start.4
  809.2 12.2 copy-start.1
  823.6 13.7 copy-start.3
  826.9 10.4 copy-start
  849.3 11.9 copy-start.4
  849.3 12.2 copy-start.1
  863.7 13.7 copy-start.3
  889.5 11.9 copy-start.4
  889.5 12.3 copy-start.1
  903.9 13.7 copy-start.3
  929.6 11.9 copy-start.4
  929.6 12.3 copy-start.1
  944.1 13.7 copy-start.3
  969.8 11.8 copy-start.4
  969.8 12.2 copy-start.1
  984.2 13.7 copy-start.3
  1009.9 11.8 copy-start.4
  1009.9 12.2 copy-start.1
  1024.8 38.1 %reduce-scatter.9.cloned.1.call-start = ((), (), s32[]{:S(2)}) async-start(), calls=%async_computation.11 | async-start | bytes 245760 | tf_op jit(solution)/shard_map/reduce_scatter | solution.py:210
  1026.6 269.9 %reduce-scatter.13.cloned.1.call-start = ((), (), s32[]{:S(2)}) async-start(), calls=%async_computation.13 | async-start | bytes 1081344 | tf_op jit(solution)/shard_map/reduce_scatter | solution.py:241
  1035.8 298.5 %reduce-scatter.19.cloned.1.call-start = ((), (), s32[]{:S(2)}) async-start(), calls=%async_computation.16 | async-start | bytes 1081344 | tf_op jit(solution)/shard_map/reduce_scatter | solution.py:244
  1047.1 420.7 %reduce-scatter.17.cloned.1.call-start = ((), (), s32[]{:S(2)}) async-start(), calls=%async_computation.15 | async-start | bytes 1081344 | tf_op jit(solution)/shard_map/reduce_scatter | solution.py:243
  1060.6 540.8 %reduce-scatter.15.cloned.1.call-start = ((), (), s32[]{:S(2)}) async-start(), calls=%async_computation.14 | async-start | bytes 1081344 | tf_op jit(solution)/shard_map/reduce_scatter | solution.py:242
  1076.2 23.3 %copy-start.22 = (bf16[16,512]{1,0:T(8,128)(2,1)S(1)}, bf16[16,512]{1,0:T(8,128)(2,1)}, u32[]{:S(2)}) copy-start(bf16[16,512]{1,0:T(8,128)(2,1)} %param.20) | copy-start | bytes 49156
  1076.2 665.0 %reduce-scatter.21.cloned.1.call-start = ((), (), s32[]{:S(2)}) async-start(), calls=%async_computation.17 | async-start | bytes 4325376 | tf_op jit(solution)/shard_map/reduce_scatter | solution.py:245
  1099.4 781.7 %reduce-scatter.23.cloned.1.call-start = ((), (), s32[]{:S(2)}) async-start(), calls=%async_computation.18 | async-start | bytes 4325376 | tf_op jit(solution)/shard_map/reduce_scatter | solution.py:246
  1141.6 21.3 %copy-start.19 = (f32[3,2,8,128]{3,1,2,0:T(2,128)S(1)}, f32[3,2,8,128]{3,1,2,0:T(2,128)}, u32[]{:S(2)}) copy-start(f32[3,2,8,128]{3,1,2,0:T(2,128)} %copy-done.17) | copy-start | bytes 73732
  1141.6 21.3 %copy-start.27 = (bf16[2048,512]{1,0:T(8,128)(2,1)S(1)}, bf16[2048,512]{1,0:T(8,128)(2,1)}, u32[]{:S(2)}) copy-start(bf16[2048,512]{1,0:T(8,128)(2,1)} %all-gather.5.cloned.1.call-done) | copy-start | bytes 6291460
  1162.9 21.6 %copy-start.10 = (bf16[512,512]{1,0:T(8,128)(2,1)S(1)}, bf16[512,512]{1,0:T(8,128)(2,1)}, u32[]{:S(2)}) copy-start(bf16[512,512]{1,0:T(8,128)(2,1)} %copy-done.9) | copy-start | bytes 1572868
  1221.7 20.3 %copy-start.25 = (f32[512]{0:T(512)S(1)}, f32[512]{0:T(512)}, u32[]{:S(2)}) copy-start(f32[512]{0:T(512)} %get-tuple-element.256) | copy-start | bytes 6148
  1221.7 58.4 %copy-start.16 = (f32[3,2,8,128]{3,1,2,0:T(2,128)S(1)}, f32[3,2,8,128]{3,1,2,0:T(2,128)}, u32[]{:S(2)}) copy-start(f32[3,2,8,128]{3,1,2,0:T(2,128)} %copy-done.15) | copy-start | bytes 73732
  (24 other events, 177.4 us)
Sparse Core Ops, SparseCore 0:
  10.9 59.7 all-gather.2
  73.6 56.3 all-gather.4
  1025.0 15.8 reduce-scatter.10
  1043.1 19.7 reduce-scatter.8
  1065.5 134.9 reduce-scatter.12
  1203.3 130.8 reduce-scatter.18
  1337.1 130.7 reduce-scatter.16
  1470.7 130.6 reduce-scatter.14
  1604.3 136.9 reduce-scatter.20
  1743.9 137.1 reduce-scatter.22
